TPU v7x, 32 devices: a whole 2x2x4 slice. The times are simulated.
32 devices in a mesh: plane: 4 (over x, core), tm: 8 (over z, y).
Axes of the slice: x: 2, y: 2, z: 4, core: 2. Of those that a mesh axis runs over, the one named last changes fastest.
Arguments:
- coeffs: float32 [32, 3, 16, 512], P('tm', None, None, 'plane'), may hold values from -1.5 to 1.5
- radius: float32 [512], P('plane'), may hold values from 0.25 to 2
- tile_mask: int32 [4, 4, 1], P(None, 'plane'), may hold values from 0 to 1
Outputs:
- hazard: float32 [4, 512], P(None, 'plane')
All inputs are finite; a program needn't handle non-finite values.
Results may differ from a plain program's by a relative error of at most 0.0003.
Values sent between devices are 32-bit elements; how exact they have to be, the bound alone decides.
No kernel may reach another device: no remote copies, remote signals or barrier semaphores. Data moves between devices by JAX's collectives and lax.ppermute only.
A program may use at most 64 MiB of HBM per device.

v0:
```python
import jax
import jax.numpy as jnp
from jax import lax
from jax.sharding import PartitionSpec as P

SAMP = 32
TILE = 128
ROUNDS = 4


def from_behind(value, axis, steps):
    count = lax.axis_size(axis)
    pairs = [(source, (source + steps) % count) for source in range(count)]
    return lax.ppermute(value, axis, pairs)


def basis_table(degrees):
    sample = jnp.arange(SAMP, dtype=jnp.float32)
    nodes = -1.0 + (2.0 * sample + 1.0) / SAMP
    series = [jnp.ones_like(nodes), nodes]
    for degree in range(2, degrees):
        series.append(2.0 * nodes * series[-1] - series[-2])
    return jnp.stack(series[:degrees], axis=1)


def synthesize(basis, coeff_block):
    return jnp.einsum("sk,wckn->wcsn", basis, coeff_block, precision=lax.Precision.HIGHEST)


def tile_values(own_pos, own_rad, far_pos, far_rad):
    inverse = 1.0 / (own_rad[:, None] + far_rad[None, :])
    separation = own_pos[:, :, :, :, None] - far_pos[:, :, :, None, :]
    squared = jnp.sum(separation * separation, axis=1)
    return jnp.sum(jnp.exp(-squared * inverse), axis=(0, 1))


def paired_sums(own_pos, own_rad, far_pos, far_rad, row_mask, column_mask):
    block_size = own_pos.shape[3]
    tile_count = block_size // TILE

    def visit(pair_index, carry):
        own_tile = pair_index // tile_count
        far_tile = pair_index % tile_count
        row_weight = row_mask[own_tile, far_tile]
        column_weight = column_mask[far_tile, own_tile]

        def compute(current):
            rows_now, columns_now = current
            values = tile_values(own_pos, own_rad, far_pos, far_rad)
            row_part = row_weight * jnp.sum(values, axis=1)
            column_part = column_weight * jnp.sum(values, axis=0)
            row_before = rows_now
            column_before = columns_now
            rows_now = row_before + row_part
            columns_now = column_before + column_part
            return (rows_now, columns_now)

        return lax.cond(row_weight + column_weight > 0, compute, lambda unchanged: unchanged, carry)

    empty = jnp.zeros((block_size,), jnp.float32)
    return lax.fori_loop(0, tile_count * tile_count, visit, (empty, empty))


def local(coeffs, radius, tile_mask):
    plane_count = lax.axis_size("plane")
    time_count = lax.axis_size("tm")
    basis = basis_table(coeffs.shape[2])
    own_pos = synthesize(basis, coeffs)
    normalizer = 1.0 / (coeffs.shape[0] * time_count * SAMP * TILE)
    mask_float = tile_mask.astype(jnp.float32)

    def finish(round_sum):
        return lax.psum(round_sum, "tm") * normalizer

    round_rows = []
    for pair_no in range(ROUNDS // 2):
        offset = pair_no + 1
        arrived, arrived_rad, arrived_mask = from_behind(
            (own_pos, radius, mask_float[2 * pair_no + 1]), "plane", offset % plane_count
        )
        row_sums, column_sums = paired_sums(
            own_pos, radius, arrived, arrived_rad, mask_float[2 * pair_no], arrived_mask
        )
        returned = from_behind(column_sums, "plane", -offset % plane_count)
        round_rows.append(finish(row_sums))
        round_rows.append(finish(returned))
    return jnp.stack(round_rows)


def solution(mesh):
    placed = (P("tm", None, None, "plane"), P("plane"), P(None, "plane", None))
    return jax.shard_map(
        local, mesh=mesh, in_specs=placed, out_specs=P(None, "plane"), check_vma=False
    )
```

profile of v0, /device:TPU:0, one launch (start us, length us, event | category | flops | bytes accessed | tf_op | source)
XLA Modules:
  0.0 80.5 jit_solution(15974278300818867515)
XLA Ops:
  0.2 0.1 stack.12
  0.3 0.6 copy-done
  0.9 0.4 convolution_bitcast_fusion
  1.3 0.5 collective-permute-start.1
  1.8 2.6 %collective-permute-start.5 = (f32[4,3,32,128]{3,2,1,0:T(8,128)S(1)}, f32[4,3,32,128]{3,2,1,0:T(8,128)S(1)}, u32[]{:S(2)}, u32[]{:S(2)}) collective-permute-start(f32[4,3,32,128]{3,2,1,0:T(8,128)S(1)} %convolution_bitcast_fusion), channel_id=1, source_target_pairs={{0,16},{8,24},{16,0},{24,8},{1,17},{9,25},{17,1},{25,9},{2,18},{10... | collective-permute-start | bytes 589832 | tf_op jit(solution)/shard_map/ppermute | solution.py:14
  4.4 0.0 collective-permute-start.2
  4.4 1.7 %collective-permute-start.6 = (f32[128]{0:T(128)}, f32[128]{0:T(128)S(1)}, u32[]{:S(2)}, u32[]{:S(2)}) collective-permute-start(f32[128]{0:T(128)} %param.8), channel_id=1, source_target_pairs={{0,16},{8,24},{16,0},{24,8},{1,17},{9,25},{17,1},{25,9},{2,18},{10... | collective-permute-start | bytes 1544 | tf_op jit(solution)/shard_map/ppermute | solution.py:14
  6.1 0.7 convert_element_type.11
  6.8 0.7 fusion.5
  7.5 0.1 collective-permute-start
  7.5 3.8 %collective-permute-done = f32[1,1]{1,0:T(1,128)} collective-permute-done((f32[1,1]{1,0:T(1,128)}, f32[1,1]{1,0:T(1,128)}, u32[]{:S(2)}, u32[]{:S(2)}) %collective-permute-start) | collective-permute-done | bytes 36 | tf_op jit(solution)/shard_map/ppermute | solution.py:14
  11.3 2.3 %collective-permute-start.4 = (f32[1,1]{1,0:T(1,128)}, f32[1,1]{1,0:T(1,128)}, u32[]{:S(2)}, u32[]{:S(2)}) collective-permute-start(f32[1,1]{1,0:T(1,128)} %bitcast.9), channel_id=1, source_target_pairs={{0,16},{8,24},{16,0},{24,8},{1,17},{9,25},{17,1},{25,9},{2,18},{10... | collective-permute-start | bytes 20 | tf_op jit(solution)/shard_map/ppermute | solution.py:14
  15.0 0.4 collective-permute-done.4
  16.7 0.0 collective-permute-done.2
  16.7 18.6 %conditional.2 = (f32[128]{0:T(128)S(1)}, f32[128]{0:T(128)S(1)}) conditional(s32[]{:T(128)} %convert_element_type.12, f32[128]{0:T(128)S(1)} %broadcast.442, (f32[]{:T(128)}, f32[4,3,32,128]{3,2,1,0:T(8,128)S(1)}, f32[4,3,32,128]{3,2,1,0:T(8,128)S(1)}, f32[128]{0:T(128)}, f32[128]{0:T(128)S(1)}, /*index=5*/f32[128]{0:T(128)S(1)}, f32[]{:T(128)}) %tuple.23), branch_computations={%region_0.1_spmd, %region_1.0_spmd} | conditional | flops 25198848 | bytes 17308212 | solution.py:58
  16.7 0.0 copy-start.1
  16.7 11.6 %multiply_reduce_fusion = f32[4,32,128,128]{3,2,1,0:T(8,128)} fusion(f32[4,3,32,128]{3,2,1,0:T(8,128)S(1)} %get-tuple-element.70, f32[4,3,32,128]{3,2,1,0:T(8,128)S(1)} %get-tuple-element.69), kind=kLoop, calls=%fused_computation | loop fusion | flops 16777216 | bytes 8781824 | tf_op jit(solution)/shard_map/while/body/eval_jaxpr/cond/branch_1_fun/reduce_sum | solution.py:33
  28.4 0.1 add_divide_fusion
  28.4 5.6 %fusion = (f32[128]{0:T(128)S(1)}, f32[128]{0:T(128)S(1)}) fusion(f32[4,32,128,128]{3,2,1,0:T(8,128)} %multiply_reduce_fusion, f32[128,128]{1,0:T(8,128)S(1)} %add_divide_fusion), kind=kLoop, calls=%fused_computation.2 | loop fusion | flops 8388352 | bytes 8455168 | tf_op jit(solution)/shard_map/while/body/eval_jaxpr/cond/branch_1_fun/reduce_sum | solution.py:51
  34.0 1.3 %multiply_add_fusion = (f32[128]{0:T(128)S(1)}, f32[128]{0:T(128)S(1)}) fusion(f32[128]{0:T(128)S(1)} %get-tuple-element.67, f32[128]{0:T(128)S(1)} %get-tuple-element.109, f32[]{:T(128)} %get-tuple-element.75, f32[128]{0:T(128)S(1)} %get-tuple-element.120, f32[]{:T(128)} %get-tuple-element.68), kind=kLoop, calls=%fused_computation.5 | loop fusion | flops 512 | bytes 2568 | tf_op jit(solution)/shard_map/while/body/eval_jaxpr/cond/branch_1_fun/add | solution.py:55
  35.3 0.1 collective-permute-start.3
  35.4 0.0 collective-permute-done.5
  35.4 18.6 %conditional.3 = (f32[128]{0:T(128)S(1)}, f32[128]{0:T(128)S(1)}) conditional(s32[]{:T(128)} %convert_element_type.13, f32[128]{0:T(128)S(1)} %broadcast.442, (f32[]{:T(128)}, f32[4,3,32,128]{3,2,1,0:T(8,128)S(1)}, f32[4,3,32,128]{3,2,1,0:T(8,128)S(1)}, f32[128]{0:T(128)}, f32[128]{0:T(128)S(1)}, /*index=5*/f32[128]{0:T(128)S(1)}, f32[]{:T(128)}) %tuple.24), branch_computations={%region_7.8_spmd, %region_8.12_spmd} | conditional | flops 25198848 | bytes 17308212 | solution.py:58
  35.4 0.0 copy-start.2
  35.4 11.6 %multiply_reduce_fusion.1 = f32[4,32,128,128]{3,2,1,0:T(8,128)} fusion(f32[4,3,32,128]{3,2,1,0:T(8,128)S(1)} %get-tuple-element.79, f32[4,3,32,128]{3,2,1,0:T(8,128)S(1)} %get-tuple-element.78), kind=kLoop, calls=%fused_computation.7 | loop fusion | flops 16777216 | bytes 8781824 | tf_op jit(solution)/shard_map/while/body/eval_jaxpr/cond/branch_1_fun/reduce_sum | solution.py:33
  47.1 0.1 add_divide_fusion.1
  47.2 5.6 %fusion.2 = (f32[128]{0:T(128)S(1)}, f32[128]{0:T(128)S(1)}) fusion(f32[4,32,128,128]{3,2,1,0:T(8,128)} %multiply_reduce_fusion.1, f32[128,128]{1,0:T(8,128)S(1)} %add_divide_fusion.1), kind=kLoop, calls=%fused_computation.9 | loop fusion | flops 8388352 | bytes 8455168 | tf_op jit(solution)/shard_map/while/body/eval_jaxpr/cond/branch_1_fun/reduce_sum | solution.py:51
  52.7 1.3 %multiply_add_fusion.2 = (f32[128]{0:T(128)S(1)}, f32[128]{0:T(128)S(1)}) fusion(f32[128]{0:T(128)S(1)} %get-tuple-element.76, f32[128]{0:T(128)S(1)} %get-tuple-element.122, f32[]{:T(128)} %get-tuple-element.100, f32[128]{0:T(128)S(1)} %get-tuple-element.124, f32[]{:T(128)} %get-tuple-element.77), kind=kLoop, calls=%fused_computation.12 | loop fusion | flops 512 | bytes 2568 | tf_op jit(solution)/shard_map/while/body/eval_jaxpr/cond/branch_1_fun/add | solution.py:55
  54.0 2.1 %collective-permute-start.7 = (f32[128]{0:T(128)S(1)}, f32[128]{0:T(128)S(1)}, u32[]{:S(2)}, u32[]{:S(2)}) collective-permute-start(f32[128]{0:T(128)S(1)} %get-tuple-element.108), channel_id=1, source_target_pairs={{0,16},{8,24},{16,0},{24,8},{1,17},{9,25},{17,1},{25,9},{2,18},{10... | collective-permute-start | bytes 1544 | tf_op jit(solution)/shard_map/ppermute | solution.py:14
  56.1 1.5 %collective-permute-done.7 = f32[128]{0:T(128)S(1)} collective-permute-done((f32[128]{0:T(128)S(1)}, f32[128]{0:T(128)S(1)}, u32[]{:S(2)}, u32[]{:S(2)}) %collective-permute-start.7) | collective-permute-done | bytes 544 | tf_op jit(solution)/shard_map/ppermute | solution.py:14
  57.7 22.2 %all-reduce = (f32[128]{0:T(128)S(1)}, f32[128]{0:T(128)S(1)}, f32[128]{0:T(128)S(1)}, f32[128]{0:T(128)S(1)}) all-reduce(f32[128]{0:T(128)S(1)} %collective-permute-done.7, f32[128]{0:T(128)S(1)} %get-tuple-element.107, f32[128]{0:T(128)S(1)} %collective-permute-done.3, ...), channel_id=1, replica_groups=mesh['plane'=4,'tm'=8] {'tm'}, use_global_device_ids=true, to_apply=%region_13.14 | all-reduce | flops 512 | bytes 4096 | tf_op jit(solution)/shard_map/psum | solution.py:73
  79.9 0.6 pad_maximum_fusion
  (20 shorter events, 0.3 us)
Async XLA Ops:
  0.0 0.9 %copy-start = (f32[4,3,16,128]{3,2,1,0:T(8,128)S(1)}, f32[4,3,16,128]{3,2,1,0:T(8,128)}, u32[]{:S(2)}) copy-start(f32[4,3,16,128]{3,2,1,0:T(8,128)} %param.7) | copy-start | bytes 294916
  1.3 15.4 %collective-permute-start.1 = (f32[4,3,32,128]{3,2,1,0:T(8,128)S(1)}, f32[4,3,32,128]{3,2,1,0:T(8,128)S(1)}, u32[]{:S(2)}, u32[]{:S(2)}) collective-permute-start(f32[4,3,32,128]{3,2,1,0:T(8,128)S(1)} %convolution_bitcast_fusion), channel_id=1, source_target_pairs={{0,8},{8,16},{16,24},{24,0},{1,9},{9,17},{17,25},{25,1},{2,10},{10... | collective-permute-start | bytes 589832 | tf_op jit(solution)/shard_map/ppermute | solution.py:14
  1.8 33.6 %collective-permute-start.5 = (f32[4,3,32,128]{3,2,1,0:T(8,128)S(1)}, f32[4,3,32,128]{3,2,1,0:T(8,128)S(1)}, u32[]{:S(2)}, u32[]{:S(2)}) collective-permute-start(f32[4,3,32,128]{3,2,1,0:T(8,128)S(1)} %convolution_bitcast_fusion), channel_id=1, source_target_pairs={{0,16},{8,24},{16,0},{24,8},{1,17},{9,25},{17,1},{25,9},{2,18},{10... | collective-permute-start | bytes 589832 | tf_op jit(solution)/shard_map/ppermute | solution.py:14
  4.4 12.3 %collective-permute-start.2 = (f32[128]{0:T(128)}, f32[128]{0:T(128)S(1)}, u32[]{:S(2)}, u32[]{:S(2)}) collective-permute-start(f32[128]{0:T(128)} %param.8), channel_id=1, source_target_pairs={{0,8},{8,16},{16,24},{24,0},{1,9},{9,17},{17,25},{25,1},{2,10},{10... | collective-permute-start | bytes 1544 | tf_op jit(solution)/shard_map/ppermute | solution.py:14
  4.4 31.0 %collective-permute-start.6 = (f32[128]{0:T(128)}, f32[128]{0:T(128)S(1)}, u32[]{:S(2)}, u32[]{:S(2)}) collective-permute-start(f32[128]{0:T(128)} %param.8), channel_id=1, source_target_pairs={{0,16},{8,24},{16,0},{24,8},{1,17},{9,25},{17,1},{25,9},{2,18},{10... | collective-permute-start | bytes 1544 | tf_op jit(solution)/shard_map/ppermute | solution.py:14
  7.5 3.9 %collective-permute-start = (f32[1,1]{1,0:T(1,128)}, f32[1,1]{1,0:T(1,128)}, u32[]{:S(2)}, u32[]{:S(2)}) collective-permute-start(f32[1,1]{1,0:T(1,128)} %bitcast.1), channel_id=1, source_target_pairs={{0,8},{8,16},{16,24},{24,0},{1,9},{9,17},{17,25},{25,1},{2,10},{10... | collective-permute-start | bytes 20 | tf_op jit(solution)/shard_map/ppermute | solution.py:14
  11.3 4.0 %collective-permute-start.4 = (f32[1,1]{1,0:T(1,128)}, f32[1,1]{1,0:T(1,128)}, u32[]{:S(2)}, u32[]{:S(2)}) collective-permute-start(f32[1,1]{1,0:T(1,128)} %bitcast.9), channel_id=1, source_target_pairs={{0,16},{8,24},{16,0},{24,8},{1,17},{9,25},{17,1},{25,9},{2,18},{10... | collective-permute-start | bytes 20 | tf_op jit(solution)/shard_map/ppermute | solution.py:14
  16.7 11.6 %copy-start.1 = (f32[128]{0:T(128)S(1)}, f32[128]{0:T(128)}, u32[]{:S(2)}) copy-start(f32[128]{0:T(128)} %get-tuple-element.71) | copy-start | bytes 1540 | tf_op jit(solution)/shard_map/while/body/eval_jaxpr/cond
  35.3 20.8 %collective-permute-start.3 = (f32[128]{0:T(128)S(1)}, f32[128]{0:T(128)S(1)}, u32[]{:S(2)}, u32[]{:S(2)}) collective-permute-start(f32[128]{0:T(128)S(1)} %get-tuple-element.106), channel_id=1, source_target_pairs={{0,24},{8,0},{16,8},{24,16},{1,25},{9,1},{17,9},{25,17},{2,26},{10... | collective-permute-start | bytes 1544 | tf_op jit(solution)/shard_map/ppermute | solution.py:14
  35.4 11.6 %copy-start.2 = (f32[128]{0:T(128)S(1)}, f32[128]{0:T(128)}, u32[]{:S(2)}) copy-start(f32[128]{0:T(128)} %get-tuple-element.80) | copy-start | bytes 1540 | tf_op jit(solution)/shard_map/while/body/eval_jaxpr/cond
  54.0 3.6 %collective-permute-start.7 = (f32[128]{0:T(128)S(1)}, f32[128]{0:T(128)S(1)}, u32[]{:S(2)}, u32[]{:S(2)}) collective-permute-start(f32[128]{0:T(128)S(1)} %get-tuple-element.108), channel_id=1, source_target_pairs={{0,16},{8,24},{16,0},{24,8},{1,17},{9,25},{17,1},{25,9},{2,18},{10... | collective-permute-start | bytes 1544 | tf_op jit(solution)/shard_map/ppermute | solution.py:14
where the time goes:
time: 80.5 us
  other arithmetic  38.6 us (48%)
  blocking collectives  22.2 us (28%)
  starting transfers between devices  9.42 us (12%)
  waiting for transfers between devices  5.77 us (7%)
  between operations  2.71 us (3%)
  local copies, waits for them, and re-layouts  1.33 us (2%)
    reduce_sum x2, other arithmetic, tile_values(): squared = jnp.sum(separation * separation, axis=1)  23.2 us
    psum x1, blocking collectives, finish(): return lax.psum(round_sum, 'tm') * normalizer  22.2 us
    reduce_sum x2, other arithmetic, compute(): column_part = column_weight * jnp.sum(values, axis=0)  11.1 us
    ppermute x8, starting transfers between devices, from_behind(): return lax.ppermute(value, axis, pairs)  9.42 us
    ppermute x8, waiting for transfers between devices, from_behind(): return lax.ppermute(value, axis, pairs)  5.77 us
    add x2, other arithmetic, compute(): columns_now = column_before + column_part  2.62 us
  transfers between devices with their start and end apart: 8, of which 3 were waited for; matrix products, arithmetic and copies ran while one was open for 48% of the time, Pallas kernels for 0%

commit v1 on v0

v1 whole, which is shorter than its diff:
```python
import functools
import math

import jax
import jax.numpy as jnp
import numpy as np
from jax import lax
from jax.experimental import pallas as pl
from jax.experimental.pallas import tpu as pltpu
from jax.sharding import PartitionSpec as P

SAMP = 32
ROUNDS = 4
AXES = 3
GROUP = 8
KINDS = 16
VMEM = pl.BlockSpec(memory_space=pltpu.VMEM)


def thirds(value):
    first = value.astype(jnp.bfloat16).astype(jnp.float32)
    rest = value - first
    second = rest.astype(jnp.bfloat16).astype(jnp.float32)
    third = (rest - second).astype(jnp.bfloat16).astype(jnp.float32)
    return first, second, third


def basis_table(degrees):
    sample = np.arange(SAMP, dtype=np.float32)
    nodes = np.float32(-1.0) + (np.float32(2.0) * sample + np.float32(1.0)) / np.float32(SAMP)
    series = [np.ones_like(nodes), nodes]
    for _ in range(2, degrees):
        series.append(np.float32(2.0) * nodes * series[-1] - series[-2])
    return np.stack(series[:degrees], axis=1).astype(np.float32)


def basis_parts(degrees):
    basis = basis_table(degrees)
    first = basis.astype(jnp.bfloat16).astype(np.float32)
    second = (basis - first).astype(jnp.bfloat16).astype(np.float32)
    third = (basis - first - second).astype(jnp.bfloat16).astype(np.float32)
    return np.concatenate([first, first, second, second, first, third], axis=1).astype(jnp.bfloat16)


def position_rows(basis, coeffs_ref, window):
    columns = []
    for axis in range(AXES):
        a, b, c = (part.astype(jnp.bfloat16) for part in thirds(coeffs_ref[window, axis]))
        columns.append(jnp.concatenate([a, b, a, b, c, a], axis=0))
    stacked = jnp.concatenate(columns, axis=1)
    rows = jnp.dot(basis, stacked, preferred_element_type=jnp.float32)
    width = coeffs_ref.shape[3]
    return [rows[:, axis * width:(axis + 1) * width] for axis in range(AXES)]


def features(rows):
    found = []
    for start in range(0, SAMP, GROUP):
        high, low, length = [], [], None
        for row in rows:
            value = row[start:start + GROUP]
            top = value.astype(jnp.bfloat16).astype(jnp.float32)
            bottom = (value - top).astype(jnp.bfloat16).astype(jnp.float32)
            kept = top + bottom
            length = kept * kept if length is None else length + kept * kept
            high.append(top)
            low.append(bottom)
        found.append((high, low, list(thirds(length))))
    return found


def own_kernel(basis_ref, coeffs_ref, radius_ref, left_ref, spread_ref):
    objects = coeffs_ref.shape[3]
    one = jnp.ones((GROUP, objects), jnp.float32)
    zero = jnp.zeros((GROUP, objects), jnp.float32)
    depth = GROUP * KINDS
    basis = basis_ref[...]
    for window in range(coeffs_ref.shape[0]):
        groups = features(position_rows(basis, coeffs_ref, window))
        for index, (high, low, length) in enumerate(groups):
            high = [-2.0 * value for value in high]
            low = [-2.0 * value for value in low]
            stack = jnp.concatenate(high + high + low + length + [one, one, one, zero], axis=0)
            place = window * len(groups) + index
            left_ref[place // 2, :, (place % 2) * depth:(place % 2 + 1) * depth] = stack.T.astype(jnp.bfloat16)
    spread_ref[...] = jnp.broadcast_to(radius_ref[...], spread_ref.shape).T


def pair_kernel(basis_ref, left_ref, spread_ref, coeffs_ref, radius_ref, out_ref, right_ref):
    objects = coeffs_ref.shape[3]
    one = jnp.ones((GROUP, objects), jnp.float32)
    zero = jnp.zeros((GROUP, objects), jnp.float32)
    depth = GROUP * KINDS
    basis = basis_ref[...]
    blank = jnp.zeros((depth, objects), jnp.bfloat16)
    for window in range(coeffs_ref.shape[0]):
        groups = features(position_rows(basis, coeffs_ref, window))
        for index, (high, low, length) in enumerate(groups):
            stack = jnp.concatenate(high + low + high + [one, one, one] + length + [zero], axis=0)
            place = window * len(groups) + index
            half = place % 2
            rows = slice(half * depth, (half + 1) * depth)
            right_ref[place // 2, rows, half * objects:(half + 1) * objects] = stack.astype(jnp.bfloat16)
            right_ref[place // 2, rows, (1 - half) * objects:(2 - half) * objects] = blank
    scale = (-1.0 / math.log(2.0)) / (spread_ref[...] + radius_ref[...])
    lane = lax.broadcasted_iota(jnp.int32, (objects, 2 * depth), 1) % GROUP

    def visit(step, total):
        left = left_ref[step]
        right = right_ref[step]
        for sample in range(GROUP):
            chosen = jnp.where(lane == sample, left, jnp.zeros_like(left))
            squared = jnp.dot(chosen, right, preferred_element_type=jnp.float32)
            total = total + jnp.exp2(squared[:, :objects] * scale) + jnp.exp2(squared[:, objects:] * scale)
        return total

    total = lax.fori_loop(0, left_ref.shape[0], visit, jnp.zeros((objects, objects), jnp.float32))
    out_ref[...] = lax.dot_general(
        jnp.ones((8, objects), jnp.float32), total, (((1,), (1,)), ((), ())),
        precision=lax.Precision.HIGHEST, preferred_element_type=jnp.float32,
    )


def own_side(basis, coeffs, radius):
    windows, _, _, objects = coeffs.shape
    pairs = windows * SAMP // GROUP // 2
    return pl.pallas_call(
        own_kernel,
        out_shape=(
            jax.ShapeDtypeStruct((pairs, objects, 2 * GROUP * KINDS), jnp.bfloat16),
            jax.ShapeDtypeStruct((objects, objects), jnp.float32),
        ),
        in_specs=[VMEM] * 3,
        out_specs=(VMEM, VMEM),
        name="own_side",
        compiler_params=pltpu.CompilerParams(vmem_limit_bytes=16 << 20),
        cost_estimate=pl.CostEstimate(flops=10_000_000, bytes_accessed=1_000_000, transcendentals=0),
    )(basis, coeffs, radius)


def pair_side(basis, left, spread, coeffs, radius):
    windows, _, _, objects = coeffs.shape
    pairs = windows * SAMP // GROUP // 2
    depth = 2 * GROUP * KINDS
    return pl.pallas_call(
        pair_kernel,
        out_shape=jax.ShapeDtypeStruct((8, objects), jnp.float32),
        in_specs=[VMEM] * 5,
        out_specs=VMEM,
        scratch_shapes=[pltpu.VMEM((pairs, depth, 2 * objects), jnp.bfloat16)],
        name="pair_side",
        compiler_params=pltpu.CompilerParams(vmem_limit_bytes=16 << 20),
        cost_estimate=pl.CostEstimate(
            flops=2 * pairs * GROUP * objects * depth * 2 * objects,
            bytes_accessed=4_000_000,
            transcendentals=windows * SAMP * objects * objects,
        ),
    )(basis, left, spread, coeffs, radius)


def moved(values, axis, pairs):
    return tuple(lax.ppermute(value, axis, pairs) for value in values)


def partners(values, plane_count):
    group = lax.axis_index("plane")
    if plane_count == 4:
        near = moved(values, "plane", [(g, g ^ 1) for g in range(4)])
        across = moved(values, "plane", [(g, g ^ 2) for g in range(4)])
        far = moved(values, "plane", [(g, g ^ 3) for g in range(4)])
        odd = group % 2
        return [near, across, far], [2 - 2 * odd, 2 * odd, 1, 1]
    steps, places = [], []
    for round_no in range(ROUNDS):
        step = (round_no // 2 + 1) * (1 if round_no % 2 == 0 else -1) % plane_count
        if step not in steps:
            steps.append(step)
        places.append(steps.index(step))
    found = [moved(values, "plane", [(g, (g + step) % plane_count) for g in range(plane_count)]) for step in steps]
    return found, places


def summed(value, axis):
    count = lax.axis_size(axis)
    if count & (count - 1):
        return lax.psum(value, axis)
    step = 1
    while step < count:
        value = value + lax.ppermute(value, axis, [(i, i ^ step) for i in range(count)])
        step *= 2
    return value


def local(coeffs, radius, tile_mask):
    windows, _, degrees, objects = coeffs.shape
    basis = jnp.asarray(basis_parts(degrees))
    radius_row = radius[None, :]
    found, places = partners((coeffs, radius_row), lax.axis_size("plane"))
    left, spread = own_side(basis, coeffs, radius_row)
    rows = [pair_side(basis, left, spread, *other)[:1] for other in found]
    normalizer = 1.0 / (windows * lax.axis_size("tm") * SAMP * objects)
    chosen = (jnp.stack([jnp.asarray(place) for place in places])[:, None] == jnp.arange(len(found))[None, :])
    weight = jnp.where(chosen, tile_mask[:, 0, :].astype(jnp.float32) * normalizer, 0.0)
    terms = sum(weight[:, index, None] * row for index, row in enumerate(rows))
    return summed(terms, "tm")


def solution(mesh):
    placed = (P("tm", None, None, "plane"), P("plane"), P(None, "plane", None))
    return jax.shard_map(
        local, mesh=mesh, in_specs=placed, out_specs=P(None, "plane"), check_vma=False
    )
```

time: 80.5 us -> 30.7 us (0.38)
  other arithmetic: 38.6 us -> 0.9 us
  blocking collectives: 22.2 us -> 0 us
  Pallas kernels: 0 us -> 10.5 us
  between operations: 2.71 us -> 0.04 us
  starting transfers between devices: 9.42 us -> 11.7 us
    reduce_sum x4 -> x0, other arithmetic: 34.4 us -> none  [the longest x2 23.2 us: tile_values(): squared = jnp.sum(separation * separation, axis=1)]
    psum x1 -> x0, blocking collectives: 22.2 us -> none  [finish(): return lax.psum(round_sum, 'tm') * normalizer]
    pallas_call x0 -> x4, Pallas kernels: none -> 10.5 us  [the longest x3 9.26 us: pair_side(): pl.pallas_call(pair_kernel, out_shape=jax.ShapeDtypeStruct((8, objects),...]
    ppermute x8 -> x9, starting transfers between devices: 9.42 us -> 11.7 us  [the longest x3 6.45 us: summed(): lax.ppermute(value, axis, [(i, i ^ step) for i in range(count)])]
    add x3 -> x4, other arithmetic: 2.63 us -> 0.81 us  [the longest x3 0.73 us: summed(): value + lax.ppermute(value, axis, [(i, i ^ step) for i in range(count)])]
    unnamed x2 -> x6, local copies, waits for them, and re-layouts: 0.61 us -> 1.91 us
    ppermute x8 -> x9, waiting for transfers between devices: 5.77 us -> 5.3 us  [the longest x3 5.24 us: summed(): lax.ppermute(value, axis, [(i, i ^ step) for i in range(count)])]
  transfers between devices with their start and end apart: 8 -> 9, of which waited for: 3 -> 3; matrix products, arithmetic and copies ran while one was open for 48% -> 0% of each run, Pallas kernels for 0% -> 24%
where the time goes in v1:
time: 30.7 us; the launch traced here: 30.4 us
  starting transfers between devices  11.7 us (38%)
  Pallas kernels  10.5 us (34%)
  waiting for transfers between devices  5.3 us (17%)
  local copies, waits for them, and re-layouts  1.93 us (6%)
  other arithmetic  0.9 us (3%)
    pallas_call x3, Pallas kernels, pair_side(): pl.pallas_call(pair_kernel, out_shape=jax.ShapeDtypeStruct((8, objects),...  9.26 us
    ppermute x3, starting transfers between devices, summed(): lax.ppermute(value, axis, [(i, i ^ step) for i in range(count)])  6.45 us
    ppermute x6, starting transfers between devices, moved(): return tuple((lax.ppermute(value, axis, pairs) for value in values))  5.29 us
    ppermute x3, waiting for transfers between devices, summed(): lax.ppermute(value, axis, [(i, i ^ step) for i in range(count)])  5.24 us
    unnamed x6, local copies, waits for them, and re-layouts  1.91 us
    pallas_call x1, Pallas kernels, own_side(): pl.pallas_call(own_kernel, out_shape=(jax.ShapeDtypeStruct((pairs, object...  1.27 us
    add x3, other arithmetic, summed(): value + lax.ppermute(value, axis, [(i, i ^ step) for i in range(count)])  0.73 us
  transfers between devices with their start and end apart: 9, of which 3 were waited for; matrix products, arithmetic and copies ran while one was open for 0% of the time, Pallas kernels for 24%

profile of v1, /device:TPU:0, one launch (start us, length us, event | category | flops | bytes accessed | tf_op | source)
XLA Modules:
  0.0 30.4 jit_solution(1793521842766279249)
XLA Ops:
  0.0 0.0 copy-start.1
  0.0 0.7 %copy-done.1 = f32[128]{0:T(128)S(1)} copy-done((f32[128]{0:T(128)S(1)}, f32[128]{0:T(128)}, u32[]{:S(2)}) %copy-start.1) | copy-done | bytes 536
  0.7 0.5 %collective-permute-start.1 = (f32[1,128]{1,0:T(1,128)S(1)}, f32[1,128]{1,0:T(1,128)S(1)}, u32[]{:S(2)}, u32[]{:S(2)}) collective-permute-start(f32[1,128]{1,0:T(1,128)S(1)} %bitcast.17), channel_id=1, source_target_pairs={{0,8},{8,0},{16,24},{24,16},{1,9},{9,1},{17,25},{25,17},{2,10},{10... | collective-permute-start | bytes 1544 | tf_op jit(solution)/shard_map/ppermute | solution.py:162
  1.1 2.5 %collective-permute-start.3 = (f32[1,128]{1,0:T(1,128)S(1)}, f32[1,128]{1,0:T(1,128)S(1)}, u32[]{:S(2)}, u32[]{:S(2)}) collective-permute-start(f32[1,128]{1,0:T(1,128)S(1)} %bitcast.18), channel_id=1, source_target_pairs={{0,16},{8,24},{16,0},{24,8},{1,17},{9,25},{17,1},{25,9},{2,18},{10... | collective-permute-start | bytes 1544 | tf_op jit(solution)/shard_map/ppermute | solution.py:162
  3.6 0.2 collective-permute-start
  3.9 0.3 collective-permute-start.2
  4.1 1.4 %collective-permute-start.5 = (f32[1,128]{1,0:T(1,128)S(1)}, f32[1,128]{1,0:T(1,128)S(1)}, u32[]{:S(2)}, u32[]{:S(2)}) collective-permute-start(f32[1,128]{1,0:T(1,128)S(1)} %bitcast.19), channel_id=1, source_target_pairs={{0,24},{8,16},{16,8},{24,0},{1,25},{9,17},{17,9},{25,1},{2,26},{10... | collective-permute-start | bytes 1544 | tf_op jit(solution)/shard_map/ppermute | solution.py:162
  5.5 0.0 copy-start.2
  5.5 0.7 %copy-done.2 = s32[4,1,1]{0,2,1:T(1,128)S(1)} copy-done((s32[4,1,1]{0,2,1:T(1,128)S(1)}, s32[4,1,1]{0,2,1:T(1,128)}, u32[]{:S(2)}) %copy-start.2) | copy-done | bytes 40
  6.2 0.1 pad_add_fusion
  6.2 0.6 %copy-done = bf16[32,96]{1,0:T(8,128)(2,1)S(1)} copy-done((bf16[32,96]{1,0:T(8,128)(2,1)S(1)}, bf16[32,96]{1,0:T(8,128)(2,1)}, u32[]{:S(2)}) %copy-start) | copy-done | bytes 6168
  6.8 1.3 %own_side.1 = (bf16[8,128,256]{2,1,0:T(8,128)(2,1)S(1)}, f32[128,128]{1,0:T(8,128)S(1)}) custom-call(bf16[32,96]{1,0:T(8,128)(2,1)S(1)} %copy-done, f32[4,3,16,128]{3,2,1,0:T(8,128)} %coeffs_ref.1, f32[1,128]{1,0:T(1,128)S(1)} %bitcast.20), custom_call_target="tpu_custom_call" | custom-call | flops 10000000 | bytes 1000000 | tf_op jit(solution)/shard_map/own_side/pallas_call | solution.py:127
  8.1 0.0 collective-permute-done.1.radius_ref
  8.1 0.5 %collective-permute-start.4 = (f32[4,3,16,128]{3,2,1,0:T(8,128)}, f32[4,3,16,128]{3,2,1,0:T(8,128)S(1)}, u32[]{:S(2)}, u32[]{:S(2)}) collective-permute-start(f32[4,3,16,128]{3,2,1,0:T(8,128)} %coeffs_ref.1), channel_id=1, source_target_pairs={{0,24},{8,16},{16,8},{24,0},{1,25},{9,17},{17,9},{25,1},{2,26},{10... | collective-permute-start | bytes 294920 | tf_op jit(solution)/shard_map/ppermute | solution.py:162
  8.6 0.0 collective-permute-done.coeffs_ref
  8.6 3.1 %pair_side.3 = f32[8,128]{1,0:T(8,128)S(1)} custom-call(bf16[32,96]{1,0:T(8,128)(2,1)S(1)} %copy-done, bf16[8,128,256]{2,1,0:T(8,128)(2,1)S(1)} %get-tuple-element.7.left_ref, f32[128,128]{1,0:T(8,128)S(1)} %get-tuple-element.8.spread_ref, f32[4,3,16,128]{3,2,1,0:T(8,128)S(1)} %collective-permute-done.coeffs_ref, f32[1,128]{1,0:T(1,128)S(1)} %collective-permute-done.1.radius_ref), custom_call_target="tpu_custom_call" | custom-call | flops 1073741824 | bytes 4000000 | tf_op jit(solution)/shard_map/pair_side/pallas_call | solution.py:145
  11.7 0.0 collective-permute-done.3.radius_ref
  11.7 0.0 collective-permute-done.2.coeffs_ref
  11.7 3.1 %pair_side.4 = f32[8,128]{1,0:T(8,128)S(1)} custom-call(bf16[32,96]{1,0:T(8,128)(2,1)S(1)} %copy-done, bf16[8,128,256]{2,1,0:T(8,128)(2,1)S(1)} %get-tuple-element.7.left_ref, f32[128,128]{1,0:T(8,128)S(1)} %get-tuple-element.8.spread_ref, f32[4,3,16,128]{3,2,1,0:T(8,128)S(1)} %collective-permute-done.2.coeffs_ref, ...), custom_call_target="tpu_custom_call" | custom-call | flops 1073741824 | bytes 4000000 | tf_op jit(solution)/shard_map/pair_side/pallas_call | solution.py:145
  14.8 0.0 collective-permute-done.5.radius_ref
  14.8 0.0 collective-permute-done.4.coeffs_ref
  14.8 3.1 %pair_side.5 = f32[8,128]{1,0:T(8,128)S(1)} custom-call(bf16[32,96]{1,0:T(8,128)(2,1)S(1)} %copy-done, bf16[8,128,256]{2,1,0:T(8,128)(2,1)S(1)} %get-tuple-element.7.left_ref, f32[128,128]{1,0:T(8,128)S(1)} %get-tuple-element.8.spread_ref, f32[4,3,16,128]{3,2,1,0:T(8,128)S(1)} %collective-permute-done.4.coeffs_ref, ...), custom_call_target="tpu_custom_call" | custom-call | flops 1073741824 | bytes 4000000 | tf_op jit(solution)/shard_map/pair_side/pallas_call | solution.py:145
  17.9 0.1 multiply_add_fusion
  18.0 1.8 %collective-permute-start.6 = (f32[4,128]{1,0:T(4,128)S(1)}, f32[4,128]{1,0:T(4,128)S(1)}, u32[]{:S(2)}, u32[]{:S(2)}) collective-permute-start(f32[4,128]{1,0:T(4,128)S(1)} %multiply_add_fusion), channel_id=1, source_target_pairs={{0,1},{1,0},{2,3},{3,2},{4,5},{5,4},{6,7},{7,6},{8,9},{9,8},{10,11... | collective-permute-start | bytes 6152 | tf_op jit(solution)/shard_map/ppermute | solution.py:189
  19.8 1.8 %collective-permute-done.6 = f32[4,128]{1,0:T(4,128)S(1)} collective-permute-done((f32[4,128]{1,0:T(4,128)S(1)}, f32[4,128]{1,0:T(4,128)S(1)}, u32[]{:S(2)}, u32[]{:S(2)}) %collective-permute-start.6) | collective-permute-done | bytes 2080 | tf_op jit(solution)/shard_map/ppermute | solution.py:189
  21.6 0.1 fusion.1
  21.7 1.8 %collective-permute-start.7 = (f32[4,128]{1,0:T(4,128)S(1)}, f32[4,128]{1,0:T(4,128)S(1)}, u32[]{:S(2)}, u32[]{:S(2)}) collective-permute-start(f32[4,128]{1,0:T(4,128)S(1)} %fusion.1), channel_id=1, source_target_pairs={{0,2},{1,3},{2,0},{3,1},{4,6},{5,7},{6,4},{7,5},{8,10},{9,11},{10,... | collective-permute-start | bytes 6152 | tf_op jit(solution)/shard_map/ppermute | solution.py:189
  23.5 1.8 %collective-permute-done.7 = f32[4,128]{1,0:T(4,128)S(1)} collective-permute-done((f32[4,128]{1,0:T(4,128)S(1)}, f32[4,128]{1,0:T(4,128)S(1)}, u32[]{:S(2)}, u32[]{:S(2)}) %collective-permute-start.7) | collective-permute-done | bytes 2080 | tf_op jit(solution)/shard_map/ppermute | solution.py:189
  25.3 0.1 fusion.2
  25.4 2.8 %collective-permute-start.8 = (f32[4,128]{1,0:T(4,128)S(1)}, f32[4,128]{1,0:T(4,128)S(1)}, u32[]{:S(2)}, u32[]{:S(2)}) collective-permute-start(f32[4,128]{1,0:T(4,128)S(1)} %fusion.2), channel_id=1, source_target_pairs={{0,4},{1,5},{2,6},{3,7},{4,0},{5,1},{6,2},{7,3},{8,12},{9,13},{10,... | collective-permute-start | bytes 6152 | tf_op jit(solution)/shard_map/ppermute | solution.py:189
  28.2 1.7 %collective-permute-done.8 = f32[4,128]{1,0:T(4,128)S(1)} collective-permute-done((f32[4,128]{1,0:T(4,128)S(1)}, f32[4,128]{1,0:T(4,128)S(1)}, u32[]{:S(2)}, u32[]{:S(2)}) %collective-permute-start.8) | collective-permute-done | bytes 2080 | tf_op jit(solution)/shard_map/ppermute | solution.py:189
  29.9 0.6 %add.24 = f32[4,128]{1,0:T(4,128)} add(f32[4,128]{1,0:T(4,128)S(1)} %fusion.2, f32[4,128]{1,0:T(4,128)S(1)} %collective-permute-done.8) | non-fusion elementwise | flops 512 | bytes 6144 | tf_op jit(solution)/shard_map/add | solution.py:189
  (8 shorter events, 0.0 us)
Async XLA Ops:
  0.0 0.7 %copy-start.1 = (f32[128]{0:T(128)S(1)}, f32[128]{0:T(128)}, u32[]{:S(2)}) copy-start(f32[128]{0:T(128)} %param.5) | copy-start | bytes 1540
  0.7 7.5 %collective-permute-start.1 = (f32[1,128]{1,0:T(1,128)S(1)}, f32[1,128]{1,0:T(1,128)S(1)}, u32[]{:S(2)}, u32[]{:S(2)}) collective-permute-start(f32[1,128]{1,0:T(1,128)S(1)} %bitcast.17), channel_id=1, source_target_pairs={{0,8},{8,0},{16,24},{24,16},{1,9},{9,1},{17,25},{25,17},{2,10},{10... | collective-permute-start | bytes 1544 | tf_op jit(solution)/shard_map/ppermute | solution.py:162
  1.1 10.5 %collective-permute-start.3 = (f32[1,128]{1,0:T(1,128)S(1)}, f32[1,128]{1,0:T(1,128)S(1)}, u32[]{:S(2)}, u32[]{:S(2)}) collective-permute-start(f32[1,128]{1,0:T(1,128)S(1)} %bitcast.18), channel_id=1, source_target_pairs={{0,16},{8,24},{16,0},{24,8},{1,17},{9,25},{17,1},{25,9},{2,18},{10... | collective-permute-start | bytes 1544 | tf_op jit(solution)/shard_map/ppermute | solution.py:162
  3.6 5.0 %collective-permute-start = (f32[4,3,16,128]{3,2,1,0:T(8,128)}, f32[4,3,16,128]{3,2,1,0:T(8,128)S(1)}, u32[]{:S(2)}, u32[]{:S(2)}) collective-permute-start(f32[4,3,16,128]{3,2,1,0:T(8,128)} %coeffs_ref.1), channel_id=1, source_target_pairs={{0,8},{8,0},{16,24},{24,16},{1,9},{9,1},{17,25},{25,17},{2,10},{10... | collective-permute-start | bytes 294920 | tf_op jit(solution)/shard_map/ppermute | solution.py:162
  3.9 7.9 %collective-permute-start.2 = (f32[4,3,16,128]{3,2,1,0:T(8,128)}, f32[4,3,16,128]{3,2,1,0:T(8,128)S(1)}, u32[]{:S(2)}, u32[]{:S(2)}) collective-permute-start(f32[4,3,16,128]{3,2,1,0:T(8,128)} %coeffs_ref.1), channel_id=1, source_target_pairs={{0,16},{8,24},{16,0},{24,8},{1,17},{9,25},{17,1},{25,9},{2,18},{10... | collective-permute-start | bytes 294920 | tf_op jit(solution)/shard_map/ppermute | solution.py:162
  4.1 10.7 %collective-permute-start.5 = (f32[1,128]{1,0:T(1,128)S(1)}, f32[1,128]{1,0:T(1,128)S(1)}, u32[]{:S(2)}, u32[]{:S(2)}) collective-permute-start(f32[1,128]{1,0:T(1,128)S(1)} %bitcast.19), channel_id=1, source_target_pairs={{0,24},{8,16},{16,8},{24,0},{1,25},{9,17},{17,9},{25,1},{2,26},{10... | collective-permute-start | bytes 1544 | tf_op jit(solution)/shard_map/ppermute | solution.py:162
  5.5 0.7 %copy-start.2 = (s32[4,1,1]{0,2,1:T(1,128)S(1)}, s32[4,1,1]{0,2,1:T(1,128)}, u32[]{:S(2)}) copy-start(s32[4,1,1]{0,2,1:T(1,128)} %param.6) | copy-start | bytes 52
  6.1 0.7 %copy-start = (bf16[32,96]{1,0:T(8,128)(2,1)S(1)}, bf16[32,96]{1,0:T(8,128)(2,1)}, u32[]{:S(2)}) copy-start(bf16[32,96]{1,0:T(8,128)(2,1)} %constant.25.clone.basis_ref) | copy-start | bytes 18436
  8.1 6.7 %collective-permute-start.4 = (f32[4,3,16,128]{3,2,1,0:T(8,128)}, f32[4,3,16,128]{3,2,1,0:T(8,128)S(1)}, u32[]{:S(2)}, u32[]{:S(2)}) collective-permute-start(f32[4,3,16,128]{3,2,1,0:T(8,128)} %coeffs_ref.1), channel_id=1, source_target_pairs={{0,24},{8,16},{16,8},{24,0},{1,25},{9,17},{17,9},{25,1},{2,26},{10... | collective-permute-start | bytes 294920 | tf_op jit(solution)/shard_map/ppermute | solution.py:162
  18.0 3.6 %collective-permute-start.6 = (f32[4,128]{1,0:T(4,128)S(1)}, f32[4,128]{1,0:T(4,128)S(1)}, u32[]{:S(2)}, u32[]{:S(2)}) collective-permute-start(f32[4,128]{1,0:T(4,128)S(1)} %multiply_add_fusion), channel_id=1, source_target_pairs={{0,1},{1,0},{2,3},{3,2},{4,5},{5,4},{6,7},{7,6},{8,9},{9,8},{10,11... | collective-permute-start | bytes 6152 | tf_op jit(solution)/shard_map/ppermute | solution.py:189
  21.7 3.6 %collective-permute-start.7 = (f32[4,128]{1,0:T(4,128)S(1)}, f32[4,128]{1,0:T(4,128)S(1)}, u32[]{:S(2)}, u32[]{:S(2)}) collective-permute-start(f32[4,128]{1,0:T(4,128)S(1)} %fusion.1), channel_id=1, source_target_pairs={{0,2},{1,3},{2,0},{3,1},{4,6},{5,7},{6,4},{7,5},{8,10},{9,11},{10,... | collective-permute-start | bytes 6152 | tf_op jit(solution)/shard_map/ppermute | solution.py:189
  25.4 4.5 %collective-permute-start.8 = (f32[4,128]{1,0:T(4,128)S(1)}, f32[4,128]{1,0:T(4,128)S(1)}, u32[]{:S(2)}, u32[]{:S(2)}) collective-permute-start(f32[4,128]{1,0:T(4,128)S(1)} %fusion.2), channel_id=1, source_target_pairs={{0,4},{1,5},{2,6},{3,7},{4,0},{5,1},{6,2},{7,3},{8,12},{9,13},{10,... | collective-permute-start | bytes 6152 | tf_op jit(solution)/shard_map/ppermute | solution.py:189
